TPU v7x, 32 devices: a whole 2x2x4 slice. The times are simulated.
32 devices in a mesh: crops: 2 (over y), rows: 4 (over z), chan: 2 (over x), sub: 2 (over core).
Axes of the slice: x: 2, y: 2, z: 4, core: 2. Of those that a mesh axis runs over, the one named last changes fastest.
Arguments:
- pair: bfloat16 [64, 32, 128], P(('crops', 'rows', 'sub')), parts along dimension 0, may hold values from -6 to 6
- residue_mask: int32 [64], P('crops'), parts along dimension 0, may hold values from 0 to 1, as said below
- in_gain: float32 [2, 128], replicated, may hold values from 0.1 to 1.9
- in_bias: float32 [2, 128], replicated, may hold values from -3 to 3
- projections: bfloat16 [2, 4, 128, 128], P(None, None, None, 'chan'), may hold values from -0.5 to 0.5
- gate_weight: bfloat16 [2, 128, 128], replicated, may hold values from -0.5 to 0.5
- out_gain: float32 [2, 128], replicated, may hold values from 0.1 to 1.9
- out_bias: float32 [2, 128], replicated, may hold values from -3 to 3
- out_weight: bfloat16 [2, 128, 128], replicated, may hold values from -0.5 to 0.5
Outputs:
- pair_out: bfloat16 [64, 32, 128], P(('crops', 'rows', 'sub'), 'chan'), parts along dimension 0
There are 2 independent parts, one for each index of `crops`. A program takes and returns all parts, laid end to end along the dimension named above; an argument that names none is the same for every part. Nothing has to cross between parts.
Inputs may be any that keep to these rules, and one draw needn't show every extreme that they name: `residue_mask`: residue 0 is always present and residue 32 - 1 is always a gap or padding.
All inputs are finite; a program needn't handle non-finite values.
Results may differ from a plain program's by a relative error of at most 0.012.
Values may be sent and summed in bfloat16 or wider, within the bound.
A program may use at most 64 MiB of HBM per device.

v0:
```python
import jax
import jax.numpy as jnp
from jax import lax
from jax.sharding import PartitionSpec as P

epsilon = 1e-05


def normalize(values, reduce_axis):
    centre = jnp.mean(values, axis=reduce_axis, keepdims=True)
    centred = values - centre
    spread = jnp.mean(centred * centred, axis=reduce_axis, keepdims=True)
    return centred * lax.rsqrt(spread + epsilon)


def shards(
    pair, residue_mask, in_gain, in_bias, projections, gate_weight, out_gain, out_bias, out_weight
):
    rows_block = pair.shape[0]
    length = pair.shape[1]
    chan_count = lax.axis_size("chan")
    chan_index = lax.axis_index("chan")
    quarter = length // chan_count
    row_start = lax.axis_index(("rows", "sub")) * rows_block
    mask_float = residue_mask.astype(jnp.float32)
    own_mask = lax.dynamic_slice_in_dim(mask_float, row_start, rows_block)
    pair_mask = own_mask[None, :, None] * mask_float[None, None, :]

    def project(full_rows, layer_index):
        normed = (
            normalize(full_rows.astype(jnp.float32), 2) * in_gain[layer_index]
            + in_bias[layer_index]
        ).astype(jnp.bfloat16)
        projected = jnp.einsum(
            "ikc,qch->qhik", normed, projections[layer_index], preferred_element_type=jnp.float32
        )
        left_edges = (jax.nn.sigmoid(projected[0]) * projected[1] * pair_mask).astype(jnp.bfloat16)
        right_edges = (jax.nn.sigmoid(projected[2]) * projected[3] * pair_mask).astype(jnp.bfloat16)
        return (normed, left_edges, right_edges)

    def finish(triangle, normed, residual, layer_index):
        gathered = lax.all_to_all(triangle, "chan", split_axis=2, concat_axis=0, tiled=True)
        whole_float = gathered.astype(jnp.float32)
        scaled = (
            normalize(whole_float, 0) * out_gain[layer_index][:, None, None]
            + out_bias[layer_index][:, None, None]
        ).astype(jnp.bfloat16)
        update = jnp.einsum(
            "hij,hc->ijc", scaled, out_weight[layer_index], preferred_element_type=jnp.float32
        )
        normed_part = lax.dynamic_slice_in_dim(normed, chan_index * quarter, quarter, 1)
        gating = jax.nn.sigmoid(
            jnp.einsum(
                "ijc,cd->ijd",
                normed_part,
                gate_weight[layer_index],
                preferred_element_type=jnp.float32,
            )
        )
        return (residual.astype(jnp.float32) + gating * update).astype(jnp.bfloat16)

    normed, left_edges, right_edges = project(pair, 0)
    triangle = jnp.einsum(
        "hik,hjk->hij",
        left_edges,
        lax.all_gather(right_edges, ("rows", "sub"), axis=1, tiled=True),
        preferred_element_type=jnp.float32,
    ).astype(jnp.bfloat16)
    own_quarter = lax.dynamic_slice_in_dim(pair, chan_index * quarter, quarter, 1)
    layer_one = finish(triangle, normed, own_quarter, 0)
    full_rows = lax.all_gather(layer_one, "chan", axis=1, tiled=True)
    normed, left_edges, right_edges = project(full_rows, 1)
    left_cols, right_cols = (
        lax.all_to_all(left_edges, ("rows", "sub"), split_axis=2, concat_axis=1, tiled=True),
        lax.all_to_all(right_edges, ("rows", "sub"), split_axis=2, concat_axis=1, tiled=True),
    )
    triangle = jnp.einsum(
        "hki,hkj->hij",
        left_cols,
        lax.all_gather(right_cols, ("rows", "sub"), axis=2, tiled=True),
        preferred_element_type=jnp.float32,
    )
    return finish(triangle.astype(jnp.bfloat16), normed, layer_one, 1)


def solution(mesh):
    placed = (
        P(("crops", "rows", "sub"), None, None),
        P("crops"),
        P(),
        P(),
        P(None, None, None, "chan"),
        P(),
        P(),
        P(),
        P(),
    )
    return jax.shard_map(
        shards,
        mesh=mesh,
        in_specs=placed,
        out_specs=P(("crops", "rows", "sub"), "chan", None),
        check_vma=False,
    )
```

profile of v0, /device:TPU:0, one launch (start us, length us, event | category | flops | bytes accessed | tf_op | source)
XLA Modules:
  0.0 73.9 jit_solution(12154159398881067945)
XLA Ops:
  0.0 0.6 copy-done.8
  0.7 0.1 dynamic_slice.14
  0.7 0.1 broadcast_multiply_fusion.2
  0.8 0.8 %convert_reduce_fusion.1 = f32[4,32]{1,0:T(4,128)S(1)} fusion(bf16[4,32,128]{2,1,0:T(8,128)(2,1)} %param.9), kind=kLoop, calls=%fused_computation.21 | loop fusion | flops 32640 | bytes 33280 | tf_op jit(solution)/shard_map/reduce_sum | solution.py:10
  1.7 0.0 copy-done
  1.7 0.2 fusion.18
  1.9 0.1 fusion.21
  2.0 0.2 convolution_bitcast_fusion.1
  2.2 0.1 fusion.36
  2.3 15.9 %all_gather.9 = bf16[64,32,32]{0,2,1:T(8,128)(2,1)S(1)} all-gather(bf16[64,4,32]{0,2,1:T(8,128)(2,1)S(1)} %get-tuple-element.11), channel_id=1, replica_groups=mesh['crops'=2,'rows'=4,'chan'=2,'sub'=2] {'rows','sub'}, dimensions={1}, use_global_device_ids=true | all-gather | bytes 147456 | tf_op jit(solution)/shard_map/all_gather | solution.py:66
  18.2 0.8 %copy.58 = bf16[64,32,32]{2,1,0:T(8,128)(2,1)S(1)} copy(bf16[64,32,32]{0,2,1:T(8,128)(2,1)S(1)} %all_gather.9) | data formatting | bytes 262144 | tf_op jit(solution)/shard_map/all_gather | solution.py:66
  19.0 0.1 copy.57
  19.1 0.4 convolution_convert_fusion.1
  19.5 0.1 copy.59
  19.6 0.0 copy-start.7
  19.6 0.7 reshape.162
  20.3 3.2 %all-to-all-start = ((bf16[2,2,2048]{2,1,0:T(2,128)(2,1)}), bf16[2,2,2048]{2,1,0:T(2,128)(2,1)S(1)}, u32[]{:S(2)}, u32[]{:S(2)}) async-start(bf16[2,2,2048]{2,1,0:T(2,128)(2,1)} %reshape.162), calls=%async_computation | async-start | bytes 32768 | tf_op jit(solution)/shard_map/all_to_all | solution.py:42
  23.6 0.0 copy-start.5
  23.6 0.0 copy-start.6
  23.6 0.1 fusion.7
  23.8 0.5 copy-done.5
  24.3 0.0 copy-done.6
  24.3 0.1 add.124
  24.4 0.1 mul.183
  24.5 2.9 %all-to-all-done = bf16[2,2,2048]{2,1,0:T(2,128)(2,1)S(1)} async-done(((bf16[2,2,2048]{2,1,0:T(2,128)(2,1)}), bf16[2,2,2048]{2,1,0:T(2,128)(2,1)S(1)}, u32[]{:S(2)}, u32[]{:S(2)}) %all-to-all-start) | async-done | bytes 16416 | tf_op jit(solution)/shard_map/all_to_all | solution.py:42
  27.4 0.1 reshape.163
  27.5 0.1 fusion.60
  27.6 0.2 fusion.63
  27.8 0.1 fusion.66
  27.9 0.0 copy-start.2
  28.0 0.1 convert_element_type.92
  28.1 0.7 copy-done.2
  28.8 0.1 fusion.8
  28.9 4.4 %all_gather.10 = bf16[4,32,128]{2,1,0:T(8,128)(2,1)S(1)} all-gather(bf16[4,16,128]{2,1,0:T(8,128)(2,1)S(1)} %fusion.8), channel_id=1, replica_groups=mesh['crops'=2,'rows'=4,'chan'=2,'sub'=2] {'chan'}, dimensions={1}, use_global_device_ids=true | all-gather | bytes 49152 | tf_op jit(solution)/shard_map/all_gather | solution.py:71
  33.3 0.1 convert_reduce_fusion
  33.4 0.2 fusion.14
  33.6 0.1 fusion.17
  33.7 0.2 convolution_bitcast_fusion
  33.9 0.1 fusion.24
  34.0 0.7 reshape.166
  34.7 4.7 %all-to-all-start.2 = ((bf16[8,2,512]{2,1,0:T(2,128)(2,1)}), bf16[8,2,512]{2,1,0:T(2,128)(2,1)S(1)}, u32[]{:S(2)}, u32[]{:S(2)}) async-start(bf16[8,2,512]{2,1,0:T(2,128)(2,1)} %reshape.166), calls=%async_computation.2 | async-start | bytes 32768 | tf_op jit(solution)/shard_map/all_to_all | solution.py:75
  39.4 0.1 add.136
  39.5 0.1 mul.200
  39.6 0.7 reshape.164
  40.3 4.8 %all-to-all-done.2 = bf16[8,2,512]{2,1,0:T(2,128)(2,1)S(1)} async-done(((bf16[8,2,512]{2,1,0:T(2,128)(2,1)}), bf16[8,2,512]{2,1,0:T(2,128)(2,1)S(1)}, u32[]{:S(2)}, u32[]{:S(2)}) %all-to-all-start.2) | async-done | bytes 16416 | tf_op jit(solution)/shard_map/all_to_all | solution.py:75
  45.1 3.3 %all-to-all-start.1 = ((bf16[8,2,512]{2,1,0:T(2,128)(2,1)}), bf16[8,2,512]{2,1,0:T(2,128)(2,1)S(1)}, u32[]{:S(2)}, u32[]{:S(2)}) async-start(bf16[8,2,512]{2,1,0:T(2,128)(2,1)} %reshape.164), calls=%async_computation.1 | async-start | bytes 32768 | tf_op jit(solution)/shard_map/all_to_all | solution.py:74
  48.4 0.1 reshape.167
  48.5 14.7 %all_gather.11 = bf16[64,32,32]{0,1,2:T(8,128)(2,1)S(1)} all-gather(bf16[64,32,4]{0,1,2:T(8,128)(2,1)S(1)} %bitcast.191), channel_id=1, replica_groups=mesh['crops'=2,'rows'=4,'chan'=2,'sub'=2] {'rows','sub'}, dimensions={2}, use_global_device_ids=true | all-gather | bytes 147456 | tf_op jit(solution)/shard_map/all_gather | solution.py:80
  63.2 0.8 %copy.68 = bf16[64,32,32]{1,2,0:T(8,128)(2,1)S(1)} copy(bf16[64,32,32]{0,1,2:T(8,128)(2,1)S(1)} %all_gather.11) | data formatting | bytes 262144 | tf_op jit(solution)/shard_map/all_gather | solution.py:80
  64.0 0.0 all-to-all-done.1
  64.0 0.1 reshape.165
  64.1 0.1 copy.67
  64.2 0.4 convolution_convert_fusion
  64.6 0.1 copy.69
  64.7 0.7 reshape.168
  65.4 3.2 %all-to-all-start.3 = ((bf16[2,2,2048]{2,1,0:T(2,128)(2,1)}), bf16[2,2,2048]{2,1,0:T(2,128)(2,1)S(1)}, u32[]{:S(2)}, u32[]{:S(2)}) async-start(bf16[2,2,2048]{2,1,0:T(2,128)(2,1)} %reshape.168), calls=%async_computation.3 | async-start | bytes 32768 | tf_op jit(solution)/shard_map/all_to_all | solution.py:42
  68.7 0.1 fusion.3
  68.8 3.7 %all-to-all-done.3 = bf16[2,2,2048]{2,1,0:T(2,128)(2,1)S(1)} async-done(((bf16[2,2,2048]{2,1,0:T(2,128)(2,1)}), bf16[2,2,2048]{2,1,0:T(2,128)(2,1)S(1)}, u32[]{:S(2)}, u32[]{:S(2)}) %all-to-all-start.3) | async-done | bytes 16416 | tf_op jit(solution)/shard_map/all_to_all | solution.py:42
  72.5 0.1 reshape.169
  72.6 0.1 fusion.52
  72.7 0.2 fusion.55
  72.9 0.1 fusion.58
  73.1 0.1 convert_element_type.104
  73.1 0.7 %fusion.9 = bf16[4,16,128]{2,1,0:T(8,128)(2,1)} fusion(f32[4,16,128]{2,1,0:T(8,128)S(1)} %fusion.3, bf16[128,4,16]{0,2,1:T(8,128)(2,1)S(1)} %convert_element_type.104, bf16[2,128,128]{2,1,0:T(8,128)(2,1)S(1)} %copy-done.2, bf16[4,16,128]{2,1,0:T(8,128)(2,1)S(1)} %fusion.8), kind=kOutput, calls=%fused_computation.17 | convolution fusion | flops 2129920 | bytes 114688 | tf_op jit(solution)/shard_map/hij,hc->ijc/dot_general | solution.py:48
  (28 shorter events, 0.2 us)
Async XLA Ops:
  0.0 0.7 copy-start.8
  0.0 1.9 %copy-start.3 = (f32[2,128]{1,0:T(2,128)S(1)}, f32[2,128]{1,0:T(2,128)}, u32[]{:S(2)}) copy-start(f32[2,128]{1,0:T(2,128)} %param.12) | copy-start | bytes 3076
  0.0 1.9 %copy-start.4 = (f32[2,128]{1,0:T(2,128)S(1)}, f32[2,128]{1,0:T(2,128)}, u32[]{:S(2)}) copy-start(f32[2,128]{1,0:T(2,128)} %param.11) | copy-start | bytes 3076
  0.0 1.7 %copy-start = (bf16[4,32,128]{2,1,0:T(8,128)(2,1)S(1)}, bf16[4,32,128]{2,1,0:T(8,128)(2,1)}, u32[]{:S(2)}) copy-start(bf16[4,32,128]{2,1,0:T(8,128)(2,1)} %param.9) | copy-start | bytes 98308
  0.0 2.0 %copy-start.1 = (bf16[2,4,128,64]{2,3,1,0:T(8,128)(2,1)S(1)}, bf16[2,4,128,64]{2,3,1,0:T(8,128)(2,1)}, u32[]{:S(2)}) copy-start(bf16[2,4,128,64]{2,3,1,0:T(8,128)(2,1)} %param.13) | copy-start | bytes 393220
  19.6 4.0 %copy-start.7 = (bf16[2,128,128]{2,1,0:T(8,128)(2,1)S(1)}, bf16[2,128,128]{2,1,0:T(8,128)(2,1)}, u32[]{:S(2)}) copy-start(bf16[2,128,128]{2,1,0:T(8,128)(2,1)} %param.14) | copy-start | bytes 196612
  20.3 7.1 %all-to-all-start = ((bf16[2,2,2048]{2,1,0:T(2,128)(2,1)}), bf16[2,2,2048]{2,1,0:T(2,128)(2,1)S(1)}, u32[]{:S(2)}, u32[]{:S(2)}) async-start(bf16[2,2,2048]{2,1,0:T(2,128)(2,1)} %reshape.162), calls=%async_computation | async-start | bytes 32768 | tf_op jit(solution)/shard_map/all_to_all | solution.py:42
  23.6 0.7 copy-start.5
  23.6 0.7 copy-start.6
  27.9 0.8 %copy-start.2 = (bf16[2,128,128]{2,1,0:T(8,128)(2,1)S(1)}, bf16[2,128,128]{2,1,0:T(8,128)(2,1)}, u32[]{:S(2)}) copy-start(bf16[2,128,128]{2,1,0:T(8,128)(2,1)} %param.17) | copy-start | bytes 196612
  34.7 10.3 %all-to-all-start.2 = ((bf16[8,2,512]{2,1,0:T(2,128)(2,1)}), bf16[8,2,512]{2,1,0:T(2,128)(2,1)S(1)}, u32[]{:S(2)}, u32[]{:S(2)}) async-start(bf16[8,2,512]{2,1,0:T(2,128)(2,1)} %reshape.166), calls=%async_computation.2 | async-start | bytes 32768 | tf_op jit(solution)/shard_map/all_to_all | solution.py:75
  45.1 18.9 %all-to-all-start.1 = ((bf16[8,2,512]{2,1,0:T(2,128)(2,1)}), bf16[8,2,512]{2,1,0:T(2,128)(2,1)S(1)}, u32[]{:S(2)}, u32[]{:S(2)}) async-start(bf16[8,2,512]{2,1,0:T(2,128)(2,1)} %reshape.164), calls=%async_computation.1 | async-start | bytes 32768 | tf_op jit(solution)/shard_map/all_to_all | solution.py:74
  65.4 7.1 %all-to-all-start.3 = ((bf16[2,2,2048]{2,1,0:T(2,128)(2,1)}), bf16[2,2,2048]{2,1,0:T(2,128)(2,1)S(1)}, u32[]{:S(2)}, u32[]{:S(2)}) async-start(bf16[2,2,2048]{2,1,0:T(2,128)(2,1)} %reshape.168), calls=%async_computation.3 | async-start | bytes 32768 | tf_op jit(solution)/shard_map/all_to_all | solution.py:42
where the time goes:
time: 74.4 us; the launch traced here: 73.9 us
  blocking collectives  35 us (47%)
  starting transfers between devices  14.5 us (19%)
  waiting for transfers between devices  11.4 us (15%)
  local copies, waits for them, and re-layouts  7.84 us (11%)
  other arithmetic  2.48 us (3%)
  matrix products  2.32 us (3%)
    all_gather x1, blocking collectives, shards(): lax.all_gather(right_edges, ('rows', 'sub'), axis=1, tiled=True)  15.9 us
    all_gather x1, blocking collectives, shards(): lax.all_gather(right_cols, ('rows', 'sub'), axis=2, tiled=True)  14.7 us
    all_to_all x2, waiting for transfers between devices, finish(): lax.all_to_all(triangle, 'chan', split_axis=2, concat_axis=0, tiled=True)  6.63 us
    all_to_all x2, starting transfers between devices, finish(): lax.all_to_all(triangle, 'chan', split_axis=2, concat_axis=0, tiled=True)  6.47 us
    unnamed x26, local copies, waits for them, and re-layouts  5.09 us
    all_to_all x1, waiting for transfers between devices, shards(): lax.all_to_all(right_edges, ('rows', 'sub'), split_axis=2, concat_axis=1,...  4.77 us
    all_to_all x1, starting transfers between devices, shards(): lax.all_to_all(right_edges, ('rows', 'sub'), split_axis=2, concat_axis=1,...  4.68 us
    all_gather x1, blocking collectives, shards(): full_rows = lax.all_gather(layer_one, 'chan', axis=1, tiled=True)  4.4 us
  transfers between devices with their start and end apart: 4, of which 3 were waited for; matrix products, arithmetic and copies ran while one was open for 3% of the time, Pallas kernels for 0%

commit v1 on v0

--- a/solution.py
+++ b/solution.py
@@ -4,6 +4,30 @@
 from jax.sharding import PartitionSpec as P
 
 epsilon = 1e-05
+
+
+def ring_apply(value, axis, dim, work, out_dim):
+    size, here, rows = (lax.axis_size(axis), lax.axis_index(axis), value.shape[dim])
+    right = [(i, (i + 1) % size) for i in range(size)]
+    behind = [(b, a) for a, b in right]
+    lower, upper = (lax.ppermute(value, axis, right), lax.ppermute(value, axis, behind))
+    made = work(value, here * rows)
+    length = made.shape[out_dim]
+    out = jnp.zeros((*made.shape[:out_dim], size * length, *made.shape[out_dim + 1 :]), made.dtype)
+
+    def put(out, made, holder):
+        return lax.dynamic_update_slice_in_dim(out, made, holder * length, axis=out_dim)
+
+    out = put(out, made, here)
+    for step in range(1, size // 2 + 1):
+        below, above = ((here - step) % size, (here + step) % size)
+        carried = (lower, upper)
+        if step < size // 2:
+            lower, upper = (lax.ppermute(lower, axis, right), lax.ppermute(upper, axis, behind))
+        out = put(out, work(carried[0], below * rows), below)
+        if 2 * step < size:
+            out = put(out, work(carried[1], above * rows), above)
+    return out
 
 
 def normalize(values, reduce_axis):
@@ -74,11 +98,14 @@
         lax.all_to_all(left_edges, ("rows", "sub"), split_axis=2, concat_axis=1, tiled=True),
         lax.all_to_all(right_edges, ("rows", "sub"), split_axis=2, concat_axis=1, tiled=True),
     )
-    triangle = jnp.einsum(
-        "hki,hkj->hij",
-        left_cols,
-        lax.all_gather(right_cols, ("rows", "sub"), axis=2, tiled=True),
-        preferred_element_type=jnp.float32,
+    triangle = ring_apply(
+        right_cols,
+        ("rows", "sub"),
+        2,
+        lambda part, start: jnp.einsum(
+            "hki,hkj->hij", left_cols, part, preferred_element_type=jnp.float32
+        ),
+        2,
     )
     return finish(triangle.astype(jnp.bfloat16), normed, layer_one, 1)
 

time: 74.4 us -> 86.4 us (1.16)
  waiting for transfers between devices: 11.4 us -> 28.7 us
  blocking collectives: 35 us -> 20.3 us
  starting transfers between devices: 14.5 us -> 22.1 us
  matrix products: 2.32 us -> 3.6 us
    ppermute x0 -> x7, waiting for transfers between devices: none -> 15.6 us  [the longest x3 11.9 us: ring_apply(): lax.ppermute(lower, axis, right)]
    all_gather x1 -> x0, blocking collectives: 14.7 us -> none  [shards(): lax.all_gather(right_cols, ('rows', 'sub'), axis=2, tiled=True)]
    ppermute x0 -> x7, starting transfers between devices: none -> 7.57 us  [the longest x2 3.66 us: ring_apply(): lax.ppermute(upper, axis, behind)]
    all_to_all x1, waiting for transfers between devices: 0.01 us -> 1.56 us  [shards(): lax.all_to_all(left_edges, ('rows', 'sub'), split_axis=2, concat_axis=1,...]
    dot_general x1 -> x8, matrix products: 0.37 us -> 1.65 us  [shards(): jnp.einsum('hki,hkj->hij', left_cols, part, preferred_element_type=jnp.fl...]
    dot_general x0 -> x8, local copies, waits for them, and re-layouts: none -> 0.96 us  [shards(): jnp.einsum('hki,hkj->hij', left_cols, part, preferred_element_type=jnp.fl...]
  transfers between devices with their start and end apart: 4 -> 11, of which waited for: 3 -> 9; matrix products, arithmetic and copies ran while one was open for 3% -> 4% of each run, Pallas kernels for 0% -> 0%
where the time goes in v1:
time: 86.4 us; the launch traced here: 85.8 us
  waiting for transfers between devices  28.7 us (33%)
  starting transfers between devices  22.1 us (26%)
  blocking collectives  20.3 us (23%)
  local copies, waits for them, and re-layouts  8.16 us (9%)
  matrix products  3.6 us (4%)
  other arithmetic  2.48 us (3%)
    all_gather x1, blocking collectives, shards(): lax.all_gather(right_edges, ('rows', 'sub'), axis=1, tiled=True)  15.9 us
    ppermute x3, waiting for transfers between devices, ring_apply(): lax.ppermute(lower, axis, right)  11.9 us
    all_to_all x2, waiting for transfers between devices, finish(): lax.all_to_all(triangle, 'chan', split_axis=2, concat_axis=0, tiled=True)  6.63 us
    all_to_all x2, starting transfers between devices, finish(): lax.all_to_all(triangle, 'chan', split_axis=2, concat_axis=0, tiled=True)  6.47 us
    unnamed x26, local copies, waits for them, and re-layouts  5.09 us
    all_to_all x1, waiting for transfers between devices, shards(): lax.all_to_all(right_edges, ('rows', 'sub'), split_axis=2, concat_axis=1,...  4.93 us
    all_to_all x1, starting transfers between devices, shards(): lax.all_to_all(right_edges, ('rows', 'sub'), split_axis=2, concat_axis=1,...  4.68 us
    all_gather x1, blocking collectives, shards(): full_rows = lax.all_gather(layer_one, 'chan', axis=1, tiled=True)  4.4 us
  transfers between devices with their start and end apart: 11, of which 9 were waited for; matrix products, arithmetic and copies ran while one was open for 4% of the time, Pallas kernels for 0%

profile of v1, /device:TPU:0, one launch (start us, length us, event | category | flops | bytes accessed | tf_op | source)
XLA Modules:
  0.0 85.8 jit_solution(1064110318421829122)
XLA Ops:
  0.0 0.6 copy-done.8
  0.8 0.8 convert_reduce_fusion.1
  1.7 0.2 fusion.18
  1.9 0.1 fusion.21
  2.0 0.2 convolution_bitcast_fusion.1
  2.3 15.9 %all_gather.6 = bf16[64,32,32]{0,2,1:T(8,128)(2,1)S(1)} all-gather(bf16[64,4,32]{0,2,1:T(8,128)(2,1)S(1)} %get-tuple-element.11), channel_id=1, replica_groups=mesh['crops'=2,'rows'=4,'chan'=2,'sub'=2] {'rows','sub'}, dimensions={1}, use_global_device_ids=true | all-gather | bytes 147456 | tf_op jit(solution)/shard_map/all_gather | solution.py:90
  18.2 0.8 copy.87
  19.0 0.1 copy.86
  19.1 0.4 convolution_convert_fusion
  19.5 0.1 copy.88
  19.6 0.7 reshape.162
  20.3 3.2 %all-to-all-start = ((bf16[2,2,2048]{2,1,0:T(2,128)(2,1)}), bf16[2,2,2048]{2,1,0:T(2,128)(2,1)S(1)}, u32[]{:S(2)}, u32[]{:S(2)}) async-start(bf16[2,2,2048]{2,1,0:T(2,128)(2,1)} %reshape.162), calls=%async_computation | async-start | bytes 32768 | tf_op jit(solution)/shard_map/all_to_all | solution.py:66
  23.6 0.1 fusion.7
  23.8 0.5 copy-done.5
  24.5 2.9 %all-to-all-done = bf16[2,2,2048]{2,1,0:T(2,128)(2,1)S(1)} async-done(((bf16[2,2,2048]{2,1,0:T(2,128)(2,1)}), bf16[2,2,2048]{2,1,0:T(2,128)(2,1)S(1)}, u32[]{:S(2)}, u32[]{:S(2)}) %all-to-all-start) | async-done | bytes 16416 | tf_op jit(solution)/shard_map/all_to_all | solution.py:66
  27.6 0.2 fusion.63
  27.8 0.1 fusion.66
  28.1 0.7 copy-done.2
  28.8 0.1 fusion.8
  28.9 4.4 %all_gather.7 = bf16[4,32,128]{2,1,0:T(8,128)(2,1)S(1)} all-gather(bf16[4,16,128]{2,1,0:T(8,128)(2,1)S(1)} %fusion.8), channel_id=1, replica_groups=mesh['crops'=2,'rows'=4,'chan'=2,'sub'=2] {'chan'}, dimensions={1}, use_global_device_ids=true | all-gather | bytes 49152 | tf_op jit(solution)/shard_map/all_gather | solution.py:95
  33.4 0.2 fusion.14
  33.6 0.1 fusion.17
  33.7 0.2 convolution_bitcast_fusion
  34.0 0.7 reshape.166
  34.7 4.7 %all-to-all-start.2 = ((bf16[8,2,512]{2,1,0:T(2,128)(2,1)}), bf16[8,2,512]{2,1,0:T(2,128)(2,1)S(1)}, u32[]{:S(2)}, u32[]{:S(2)}) async-start(bf16[8,2,512]{2,1,0:T(2,128)(2,1)} %reshape.166), calls=%async_computation.2 | async-start | bytes 32768 | tf_op jit(solution)/shard_map/all_to_all | solution.py:99
  39.4 0.7 reshape.164
  40.1 4.9 %all-to-all-done.2 = bf16[8,2,512]{2,1,0:T(2,128)(2,1)S(1)} async-done(((bf16[8,2,512]{2,1,0:T(2,128)(2,1)}), bf16[8,2,512]{2,1,0:T(2,128)(2,1)S(1)}, u32[]{:S(2)}, u32[]{:S(2)}) %all-to-all-start.2) | async-done | bytes 16416 | tf_op jit(solution)/shard_map/all_to_all | solution.py:99
  45.1 3.3 %all-to-all-start.1 = ((bf16[8,2,512]{2,1,0:T(2,128)(2,1)}), bf16[8,2,512]{2,1,0:T(2,128)(2,1)S(1)}, u32[]{:S(2)}, u32[]{:S(2)}) async-start(bf16[8,2,512]{2,1,0:T(2,128)(2,1)} %reshape.164), calls=%async_computation.1 | async-start | bytes 32768 | tf_op jit(solution)/shard_map/all_to_all | solution.py:98
  48.8 0.1 copy.97
  48.9 0.3 collective-permute-start
  49.3 3.3 %collective-permute-start.1 = (bf16[64,32,4]{1,2,0:T(4,128)(2,1)S(1)}, bf16[64,32,4]{1,2,0:T(4,128)(2,1)S(1)}, u32[]{:S(2)}, u32[]{:S(2)}) collective-permute-start(bf16[64,32,4]{1,2,0:T(4,128)(2,1)S(1)} %copy.97), channel_id=1, source_target_pairs={{1,0},{4,1},{5,4},{8,5},{9,8},{12,9},{13,12},{0,13},{3,2},{6,3},{7... | collective-permute-start | bytes 49160 | tf_op jit(solution)/shard_map/ppermute | solution.py:13
  52.5 1.6 %all-to-all-done.1 = bf16[8,2,512]{2,1,0:T(2,128)(2,1)S(1)} async-done(((bf16[8,2,512]{2,1,0:T(2,128)(2,1)}), bf16[8,2,512]{2,1,0:T(2,128)(2,1)S(1)}, u32[]{:S(2)}, u32[]{:S(2)}) %all-to-all-start.1) | async-done | bytes 16416 | tf_op jit(solution)/shard_map/all_to_all | solution.py:98
  54.2 0.1 copy.96
  54.3 0.2 fusion.84
  54.5 0.1 copy.98
  54.7 0.2 fusion.86
  54.9 0.1 copy.104
  55.0 0.2 fusion.85
  55.2 0.1 copy.101
  55.4 3.4 %collective-permute-start.3 = (bf16[64,32,4]{1,2,0:T(4,128)(2,1)S(1)}, bf16[64,32,4]{1,2,0:T(4,128)(2,1)S(1)}, u32[]{:S(2)}, u32[]{:S(2)}) collective-permute-start(bf16[64,32,4]{1,2,0:T(4,128)(2,1)S(1)} %collective-permute-done.1), channel_id=1, source_target_pairs={{1,0},{4,1},{5,4},{8,5},{9,8},{12,9},{13,12},{0,13},{3,2},{6,3},{7... | collective-permute-start | bytes 49160 | tf_op jit(solution)/shard_map/ppermute | solution.py:26
  58.7 1.9 %collective-permute-done.3 = bf16[64,32,4]{1,2,0:T(4,128)(2,1)S(1)} collective-permute-done((bf16[64,32,4]{1,2,0:T(4,128)(2,1)S(1)}, bf16[64,32,4]{1,2,0:T(4,128)(2,1)S(1)}, u32[]{:S(2)}, u32[]{:S(2)}) %collective-permute-start.3) | collective-permute-done | bytes 16416 | tf_op jit(solution)/shard_map/ppermute | solution.py:26
  60.6 0.2 fusion.88
  60.8 0.1 copy.108
  61.0 3.3 %collective-permute-done.2 = bf16[64,32,4]{1,2,0:T(4,128)(2,1)S(1)} collective-permute-done((bf16[64,32,4]{1,2,0:T(4,128)(2,1)S(1)}, bf16[64,32,4]{1,2,0:T(4,128)(2,1)S(1)}, u32[]{:S(2)}, u32[]{:S(2)}) %collective-permute-start.2) | collective-permute-done | bytes 16416 | tf_op jit(solution)/shard_map/ppermute | solution.py:26
  64.3 0.2 fusion.87
  64.5 0.1 copy.106
  64.6 0.3 collective-permute-start.5
  65.0 0.3 collective-permute-start.4
  65.2 1.8 %collective-permute-done.5 = bf16[64,32,4]{1,2,0:T(4,128)(2,1)S(1)} collective-permute-done((bf16[64,32,4]{1,2,0:T(4,128)(2,1)S(1)}, bf16[64,32,4]{1,2,0:T(4,128)(2,1)S(1)}, u32[]{:S(2)}, u32[]{:S(2)}) %collective-permute-start.5) | collective-permute-done | bytes 16416 | tf_op jit(solution)/shard_map/ppermute | solution.py:26
  67.0 0.2 fusion.90
  67.2 0.1 copy.112
  67.3 3.1 %collective-permute-done.4 = bf16[64,32,4]{1,2,0:T(4,128)(2,1)S(1)} collective-permute-done((bf16[64,32,4]{1,2,0:T(4,128)(2,1)S(1)}, bf16[64,32,4]{1,2,0:T(4,128)(2,1)S(1)}, u32[]{:S(2)}, u32[]{:S(2)}) %collective-permute-start.4) | collective-permute-done | bytes 16416 | tf_op jit(solution)/shard_map/ppermute | solution.py:26
  70.5 0.2 fusion.89
  70.7 0.1 copy.110
  70.9 5.5 %collective-permute-done.6 = bf16[64,32,4]{1,2,0:T(4,128)(2,1)S(1)} collective-permute-done((bf16[64,32,4]{1,2,0:T(4,128)(2,1)S(1)}, bf16[64,32,4]{1,2,0:T(4,128)(2,1)S(1)}, u32[]{:S(2)}, u32[]{:S(2)}) %collective-permute-start.6) | collective-permute-done | bytes 16416 | tf_op jit(solution)/shard_map/ppermute | solution.py:26
  76.3 0.2 fusion.91
  76.5 0.1 copy.114
  76.7 0.7 reshape.168
  77.4 3.2 %all-to-all-start.3 = ((bf16[2,2,2048]{2,1,0:T(2,128)(2,1)}), bf16[2,2,2048]{2,1,0:T(2,128)(2,1)S(1)}, u32[]{:S(2)}, u32[]{:S(2)}) async-start(bf16[2,2,2048]{2,1,0:T(2,128)(2,1)} %reshape.168), calls=%async_computation.3 | async-start | bytes 32768 | tf_op jit(solution)/shard_map/all_to_all | solution.py:66
  80.6 0.1 fusion.3
  80.8 3.7 %all-to-all-done.3 = bf16[2,2,2048]{2,1,0:T(2,128)(2,1)S(1)} async-done(((bf16[2,2,2048]{2,1,0:T(2,128)(2,1)}), bf16[2,2,2048]{2,1,0:T(2,128)(2,1)S(1)}, u32[]{:S(2)}, u32[]{:S(2)}) %all-to-all-start.3) | async-done | bytes 16416 | tf_op jit(solution)/shard_map/all_to_all | solution.py:66
  84.7 0.2 fusion.55
  84.9 0.1 fusion.58
  85.1 0.7 fusion.9
  (64 shorter events, 1.9 us)
Async XLA Ops:
  0.0 0.7 copy-start.8
  0.0 1.9 %copy-start.3 = (f32[2,128]{1,0:T(2,128)S(1)}, f32[2,128]{1,0:T(2,128)}, u32[]{:S(2)}) copy-start(f32[2,128]{1,0:T(2,128)} %param.12) | copy-start | bytes 3076
  0.0 1.9 %copy-start.4 = (f32[2,128]{1,0:T(2,128)S(1)}, f32[2,128]{1,0:T(2,128)}, u32[]{:S(2)}) copy-start(f32[2,128]{1,0:T(2,128)} %param.11) | copy-start | bytes 3076
  0.0 1.7 %copy-start = (bf16[4,32,128]{2,1,0:T(8,128)(2,1)S(1)}, bf16[4,32,128]{2,1,0:T(8,128)(2,1)}, u32[]{:S(2)}) copy-start(bf16[4,32,128]{2,1,0:T(8,128)(2,1)} %param.9) | copy-start | bytes 98308
  0.0 2.0 %copy-start.1 = (bf16[2,4,128,64]{2,3,1,0:T(8,128)(2,1)S(1)}, bf16[2,4,128,64]{2,3,1,0:T(8,128)(2,1)}, u32[]{:S(2)}) copy-start(bf16[2,4,128,64]{2,3,1,0:T(8,128)(2,1)} %param.13) | copy-start | bytes 393220
  19.6 4.0 %copy-start.7 = (bf16[2,128,128]{2,1,0:T(8,128)(2,1)S(1)}, bf16[2,128,128]{2,1,0:T(8,128)(2,1)}, u32[]{:S(2)}) copy-start(bf16[2,128,128]{2,1,0:T(8,128)(2,1)} %param.14) | copy-start | bytes 196612
  20.3 7.1 %all-to-all-start = ((bf16[2,2,2048]{2,1,0:T(2,128)(2,1)}), bf16[2,2,2048]{2,1,0:T(2,128)(2,1)S(1)}, u32[]{:S(2)}, u32[]{:S(2)}) async-start(bf16[2,2,2048]{2,1,0:T(2,128)(2,1)} %reshape.162), calls=%async_computation | async-start | bytes 32768 | tf_op jit(solution)/shard_map/all_to_all | solution.py:66
  23.6 0.7 copy-start.5
  23.6 0.7 copy-start.6
  27.9 0.8 copy-start.2
  34.7 10.3 %all-to-all-start.2 = ((bf16[8,2,512]{2,1,0:T(2,128)(2,1)}), bf16[8,2,512]{2,1,0:T(2,128)(2,1)S(1)}, u32[]{:S(2)}, u32[]{:S(2)}) async-start(bf16[8,2,512]{2,1,0:T(2,128)(2,1)} %reshape.166), calls=%async_computation.2 | async-start | bytes 32768 | tf_op jit(solution)/shard_map/all_to_all | solution.py:99
  45.1 9.0 %all-to-all-start.1 = ((bf16[8,2,512]{2,1,0:T(2,128)(2,1)}), bf16[8,2,512]{2,1,0:T(2,128)(2,1)S(1)}, u32[]{:S(2)}, u32[]{:S(2)}) async-start(bf16[8,2,512]{2,1,0:T(2,128)(2,1)} %reshape.164), calls=%async_computation.1 | async-start | bytes 32768 | tf_op jit(solution)/shard_map/all_to_all | solution.py:98
  48.9 6.1 %collective-permute-start = (bf16[64,32,4]{1,2,0:T(4,128)(2,1)S(1)}, bf16[64,32,4]{1,2,0:T(4,128)(2,1)S(1)}, u32[]{:S(2)}, u32[]{:S(2)}) collective-permute-start(bf16[64,32,4]{1,2,0:T(4,128)(2,1)S(1)} %copy.97), channel_id=1, source_target_pairs={{0,1},{1,4},{4,5},{5,8},{8,9},{9,12},{12,13},{13,0},{2,3},{3,6},{6... | collective-permute-start | bytes 49160 | tf_op jit(solution)/shard_map/ppermute | solution.py:13
  49.3 5.4 %collective-permute-start.1 = (bf16[64,32,4]{1,2,0:T(4,128)(2,1)S(1)}, bf16[64,32,4]{1,2,0:T(4,128)(2,1)S(1)}, u32[]{:S(2)}, u32[]{:S(2)}) collective-permute-start(bf16[64,32,4]{1,2,0:T(4,128)(2,1)S(1)} %copy.97), channel_id=1, source_target_pairs={{1,0},{4,1},{5,4},{8,5},{9,8},{12,9},{13,12},{0,13},{3,2},{6,3},{7... | collective-permute-start | bytes 49160 | tf_op jit(solution)/shard_map/ppermute | solution.py:13
  55.4 5.3 %collective-permute-start.3 = (bf16[64,32,4]{1,2,0:T(4,128)(2,1)S(1)}, bf16[64,32,4]{1,2,0:T(4,128)(2,1)S(1)}, u32[]{:S(2)}, u32[]{:S(2)}) collective-permute-start(bf16[64,32,4]{1,2,0:T(4,128)(2,1)S(1)} %collective-permute-done.1), channel_id=1, source_target_pairs={{1,0},{4,1},{5,4},{8,5},{9,8},{12,9},{13,12},{0,13},{3,2},{6,3},{7... | collective-permute-start | bytes 49160 | tf_op jit(solution)/shard_map/ppermute | solution.py:26
  58.7 5.6 %collective-permute-start.2 = (bf16[64,32,4]{1,2,0:T(4,128)(2,1)S(1)}, bf16[64,32,4]{1,2,0:T(4,128)(2,1)S(1)}, u32[]{:S(2)}, u32[]{:S(2)}) collective-permute-start(bf16[64,32,4]{1,2,0:T(4,128)(2,1)S(1)} %collective-permute-done), channel_id=1, source_target_pairs={{0,1},{1,4},{4,5},{5,8},{8,9},{9,12},{12,13},{13,0},{2,3},{3,6},{6... | collective-permute-start | bytes 49160 | tf_op jit(solution)/shard_map/ppermute | solution.py:26
  64.6 2.4 %collective-permute-start.5 = (bf16[64,32,4]{1,2,0:T(4,128)(2,1)S(1)}, bf16[64,32,4]{1,2,0:T(4,128)(2,1)S(1)}, u32[]{:S(2)}, u32[]{:S(2)}) collective-permute-start(bf16[64,32,4]{1,2,0:T(4,128)(2,1)S(1)} %collective-permute-done.3), channel_id=1, source_target_pairs={{1,0},{4,1},{5,4},{8,5},{9,8},{12,9},{13,12},{0,13},{3,2},{6,3},{7... | collective-permute-start | bytes 49160 | tf_op jit(solution)/shard_map/ppermute | solution.py:26
  65.0 5.5 %collective-permute-start.4 = (bf16[64,32,4]{1,2,0:T(4,128)(2,1)S(1)}, bf16[64,32,4]{1,2,0:T(4,128)(2,1)S(1)}, u32[]{:S(2)}, u32[]{:S(2)}) collective-permute-start(bf16[64,32,4]{1,2,0:T(4,128)(2,1)S(1)} %collective-permute-done.2), channel_id=1, source_target_pairs={{0,1},{1,4},{4,5},{5,8},{8,9},{9,12},{12,13},{13,0},{2,3},{3,6},{6... | collective-permute-start | bytes 49160 | tf_op jit(solution)/shard_map/ppermute | solution.py:26
  70.8 5.5 %collective-permute-start.6 = (bf16[64,32,4]{1,2,0:T(4,128)(2,1)S(1)}, bf16[64,32,4]{1,2,0:T(4,128)(2,1)S(1)}, u32[]{:S(2)}, u32[]{:S(2)}) collective-permute-start(bf16[64,32,4]{1,2,0:T(4,128)(2,1)S(1)} %collective-permute-done.4), channel_id=1, source_target_pairs={{0,1},{1,4},{4,5},{5,8},{8,9},{9,12},{12,13},{13,0},{2,3},{3,6},{6... | collective-permute-start | bytes 49160 | tf_op jit(solution)/shard_map/ppermute | solution.py:26
  77.4 7.1 %all-to-all-start.3 = ((bf16[2,2,2048]{2,1,0:T(2,128)(2,1)}), bf16[2,2,2048]{2,1,0:T(2,128)(2,1)S(1)}, u32[]{:S(2)}, u32[]{:S(2)}) async-start(bf16[2,2,2048]{2,1,0:T(2,128)(2,1)} %reshape.168), calls=%async_computation.3 | async-start | bytes 32768 | tf_op jit(solution)/shard_map/all_to_all | solution.py:66
